TPU v7x, 32 devices: a whole 2x2x4 slice. The times are simulated.
32 devices in a mesh: strike: 8 (over z, y), depth: 4 (over x, core).
Axes of the slice: x: 2, y: 2, z: 4, core: 2. Of those that a mesh axis runs over, the one named last changes fastest.
Arguments:
- velocity: float32 [3, 128, 64, 256], P(None, 'strike', 'depth'), may hold values from -6 to 6
- stress: float32 [6, 128, 64, 256], P(None, 'strike', 'depth'), may hold values from -6 to 6
- material: int32 [128, 64, 256], P('strike', 'depth'), may hold values from 0 to 3
- patch_order: int32 [48], replicated, may hold values from 0 to 47, each once
- fault_params: float32 [4, 64, 48], P(None, 'depth', 'strike'), may hold values from -5 to 5, as said below
Outputs:
- velocity_out: float32 [3, 128, 64, 256], P(None, 'strike', 'depth')
- slip_rate: float32 [64, 48], P('depth', 'strike')
Inputs may be any that keep to these rules, and one draw needn't show every extreme that they name: `fault_params`: row 0 in 0.3 to 1.2, row 1 in -0.5 to 1.5, row 2 in 1 to 3, row 3 in -5 to 5. `patch_order`: each fault column exactly once.
All inputs are finite; a program needn't handle non-finite values.
Results may differ from a plain program's by a relative error of at most 0.0003.
Values sent between devices are 32-bit elements; how exact they have to be, the bound alone decides.
A program may use at most 64 MiB of HBM per device.

v0:
```python
import jax
import jax.numpy as jnp
from jax import lax
from jax.sharding import PartitionSpec as P

NEWTON = 8
BUOY = (1.0, 0.8, 0.6, 1.25)
C_ONE = 9.0 / 8.0
C_TWO = -1.0 / 24.0


def with_halo(value, sides, width):
    for axis, dim in sides:
        size, length = (lax.axis_size(axis), value.shape[dim])
        up = [(i, (i + 1) % size) for i in range(size - 1)]
        down = [(j, i) for i, j in up]
        last = lax.slice_in_dim(value, length - width, length, axis=dim)
        first = lax.slice_in_dim(value, 0, width, axis=dim)
        before = lax.ppermute(last, axis, up)
        after = lax.ppermute(first, axis, down)
        value = jnp.concatenate([before, value, after], axis=dim)
    return value


def inverse_sinh(value):
    magnitude = jnp.log(jnp.abs(value) + jnp.sqrt(1.0 + value * value))
    return jnp.where(value < 0, -magnitude, magnitude)


def minus_padded(padded, axis):
    width = padded.shape[axis] - 4

    def part(offset):
        return lax.slice_in_dim(padded, 2 + offset, 2 + offset + width, axis=axis)

    return C_ONE * (part(0) - part(-1)) + C_TWO * (part(1) - part(-2))


def plus_padded(padded, axis):
    width = padded.shape[axis] - 4

    def part(offset):
        return lax.slice_in_dim(padded, 2 + offset, 2 + offset + width, axis=axis)

    return C_ONE * (part(1) - part(0)) + C_TWO * (part(2) - part(-1))


def pad_normal(field):
    return jnp.pad(field, ((0, 0), (0, 0), (2, 2)))


def friction(tau_trial, params):
    coef, psi, normal_stress, background = (params[0], params[1], params[2], params[3])
    tau_total = tau_trial + background
    half_q = 0.5 * jnp.exp(psi / coef)
    scale = normal_stress * coef
    rate = jnp.zeros_like(tau_total)
    for step in range(NEWTON):
        arg_val = rate * half_q
        resid = tau_total - rate - scale * inverse_sinh(arg_val)
        slope = -1.0 - scale * half_q / jnp.sqrt(1.0 + arg_val * arg_val)
        rate = rate - 0.35 * resid / slope
    return rate


def per_device(velocity, stress, material, patch_order, fault_params):
    cx, cz, ny = (stress.shape[1], stress.shape[2], stress.shape[3])
    row = ny // 2
    stacked = jnp.stack([stress[0], stress[2], stress[3], stress[4], stress[5]])
    padded = with_halo(stacked, (("strike", 1), ("depth", 2)), 2)
    x_part = padded[:, :, 2:-2]
    z_part = padded[:, 2:-2, :]
    x_sxx, x_sxy, x_sxz = (x_part[0], x_part[2], x_part[3])
    z_sxz, z_syz, z_szz = (z_part[3], z_part[4], z_part[1])
    buoyancy = jnp.zeros(material.shape, jnp.float32)
    for index in range(4):
        buoyancy = buoyancy + (material == index).astype(jnp.float32) * BUOY[index]
    dxx = minus_padded(x_sxx, 0)
    vx = velocity[0] + 0.25 * buoyancy * (
        dxx + minus_padded(pad_normal(stress[3]), 2) + minus_padded(z_sxz, 1)
    )
    vy = velocity[1] + 0.25 * buoyancy * (
        plus_padded(x_sxy, 0) + plus_padded(pad_normal(stress[1]), 2) + minus_padded(z_syz, 1)
    )
    vz = velocity[2] + 0.25 * buoyancy * (
        plus_padded(x_sxz, 0) + plus_padded(pad_normal(stress[5]), 2) + plus_padded(z_szz, 1)
    )
    fault_cols = patch_order.shape[0]
    n_strike = lax.axis_size("strike")
    strike_pos = lax.axis_index("strike")
    first_tile = n_strike // 4
    fault_tiles = fault_cols // cx
    inside = jnp.logical_and(strike_pos >= first_tile, strike_pos < first_tile + fault_tiles)
    offset = jnp.clip(strike_pos - first_tile, 0, fault_tiles - 1) * cx
    selector = (patch_order[:, None] == jnp.arange(fault_cols, dtype=jnp.int32)[None, :]).astype(
        jnp.float32
    )
    local_traction = (stress[3, :, :, row] + 0.5 * dxx[:, :, row]).T
    blank = jnp.zeros((cz, fault_cols), jnp.float32)
    masked = jnp.where(inside, local_traction, 0.0)
    owned = lax.psum_scatter(
        jnp.dot(
            lax.dynamic_update_slice(blank, masked, (jnp.int32(0), offset)),
            selector.T,
            precision=lax.Precision.HIGHEST,
            preferred_element_type=jnp.float32,
        ),
        "strike",
        scatter_dimension=1,
        tiled=True,
    )
    slip_own = friction(owned, fault_params)
    slip_all = lax.all_gather(slip_own, "strike", axis=1, tiled=True)
    slip_tile = lax.dynamic_slice(
        jnp.dot(
            slip_all, selector, precision=lax.Precision.HIGHEST, preferred_element_type=jnp.float32
        ),
        (jnp.int32(0), offset),
        (cz, cx),
    )
    slip_planar = slip_tile.T
    plus_side = vx[:, :, row]
    minus_side = vx[:, :, row - 1]
    middle = 0.5 * (plus_side + minus_side)
    vx = vx.at[:, :, row].set(jnp.where(inside, middle + 0.5 * slip_planar, plus_side))
    vx = vx.at[:, :, row - 1].set(jnp.where(inside, middle - 0.5 * slip_planar, minus_side))
    return (jnp.stack([vx, vy, vz]), slip_own)


def solution(mesh):
    return jax.shard_map(
        per_device,
        mesh=mesh,
        in_specs=(
            P(None, "strike", "depth", None),
            P(None, "strike", "depth", None),
            P("strike", "depth", None),
            P(),
            P(None, "depth", "strike"),
        ),
        out_specs=(P(None, "strike", "depth", None), P("depth", "strike")),
        check_vma=False,
    )
```

profile of v0, /device:TPU:2, one launch (start us, length us, event | category | flops | bytes accessed | tf_op | source)
XLA Modules:
  0.0 105.1 jit_solution(18227903959645477159)
XLA Ops:
  0.6 2.1 %slice_bitcast_fusion.2 = (f32[16,16,256]{2,1,0:T(8,128)}, f32[16,16,256]{2,1,0:T(8,128)S(1)}, f32[1,16,16,256]{3,2,1,0:T(8,128)S(1)}, f32[16,16,256]{2,1,0:T(8,128)S(1)}) fusion(f32[6,16,16,256]{3,2,1,0:T(8,128)} %param.10), kind=kLoop, calls=%fused_computation.87 | loop fusion | bytes 2097152 | tf_op jit(solution)/shard_map/squeeze | solution.py:80
  2.8 1.3 %collective-permute-start.1 = (f32[5,2,16,256]{3,2,1,0:T(8,128)S(1)}, f32[5,2,16,256]{3,2,1,0:T(8,128)S(1)}, u32[]{:S(2)}, u32[]{:S(2)}) collective-permute-start(f32[5,2,16,256]{3,2,1,0:T(8,128)S(1)} %get-tuple-element.42), channel_id=1, source_target_pairs={{4,0},{8,4},{12,8},{16,12},{20,16},{24,20},{28,24},{5,1},{9,5},{13... | collective-permute-start | bytes 491528 | tf_op jit(solution)/shard_map/ppermute | solution.py:20
  4.1 4.6 %collective-permute-start = (f32[5,2,16,256]{3,2,1,0:T(8,128)S(1)}, f32[5,2,16,256]{3,2,1,0:T(8,128)S(1)}, u32[]{:S(2)}, u32[]{:S(2)}) collective-permute-start(f32[5,2,16,256]{3,2,1,0:T(8,128)S(1)} %get-tuple-element.41), channel_id=1, source_target_pairs={{0,4},{4,8},{8,12},{12,16},{16,20},{20,24},{24,28},{1,5},{5,9},{9,... | collective-permute-start | bytes 491528 | tf_op jit(solution)/shard_map/ppermute | solution.py:19
  8.9 0.6 dynamic-slice.16
  10.1 0.5 collective-permute-done.1
  10.7 3.4 %collective-permute-done = f32[5,2,16,256]{3,2,1,0:T(8,128)S(1)} collective-permute-done((f32[5,2,16,256]{3,2,1,0:T(8,128)S(1)}, f32[5,2,16,256]{3,2,1,0:T(8,128)S(1)}, u32[]{:S(2)}, u32[]{:S(2)}) %collective-permute-start) | collective-permute-done | bytes 163872 | tf_op jit(solution)/shard_map/ppermute | solution.py:19
  14.3 2.1 %collective-permute-start.3 = (f32[5,20,2,256]{3,2,1,0:T(2,128)S(1)}, f32[5,20,2,256]{3,2,1,0:T(2,128)S(1)}, u32[]{:S(2)}, u32[]{:S(2)}) collective-permute-start(f32[5,20,2,256]{3,2,1,0:T(2,128)S(1)} %get-tuple-element.36), channel_id=1, source_target_pairs={{1,0},{2,1},{3,2},{5,4},{6,5},{7,6},{9,8},{10,9},{11,10},{13,12},{... | collective-permute-start | bytes 614408 | tf_op jit(solution)/shard_map/ppermute | solution.py:20
  16.3 2.3 %collective-permute-start.2 = (f32[5,20,2,256]{3,2,1,0:T(2,128)S(1)}, f32[5,20,2,256]{3,2,1,0:T(2,128)S(1)}, u32[]{:S(2)}, u32[]{:S(2)}) collective-permute-start(f32[5,20,2,256]{3,2,1,0:T(2,128)S(1)} %get-tuple-element.35), channel_id=1, source_target_pairs={{0,1},{1,2},{2,3},{4,5},{5,6},{6,7},{8,9},{9,10},{10,11},{12,13},{... | collective-permute-start | bytes 614408 | tf_op jit(solution)/shard_map/ppermute | solution.py:19
  18.7 0.9 collective-permute-done.3
  19.6 3.8 %collective-permute-done.2 = f32[5,20,2,256]{3,2,1,0:T(2,128)S(1)} collective-permute-done((f32[5,20,2,256]{3,2,1,0:T(2,128)S(1)}, f32[5,20,2,256]{3,2,1,0:T(2,128)S(1)}, u32[]{:S(2)}, u32[]{:S(2)}) %collective-permute-start.2) | collective-permute-done | bytes 204832 | tf_op jit(solution)/shard_map/ppermute | solution.py:19
  23.6 1.3 %fusion.7 = (f32[16,16,256]{2,1,0:T(8,128)S(1)}, f32[16,16,256]{2,1,0:T(8,128)S(1)}) fusion(f32[16,16,256]{2,1,0:T(8,128)S(1)} %copy-done.2, f32[16,20,256]{2,1,0:T(8,128)S(1)} %get-tuple-element.32, f32[3,16,16,256]{3,2,1,0:T(8,128)} %param.9, s32[16,16,256]{2,1,0:T(8,128)S(1)} %copy-done.1, f32[4,16,16,256]{3,2,1,0:T(8,128)S(1)} %slice.262, ...), kind=kLoop, calls=%fused_computation.24 | loop fusion | flops 2424832 | bytes 3997696 | tf_op jit(solution)/shard_map/add | solution.py:79
  25.0 0.8 fusion.108
  25.7 1.1 %copy.199 = f32[16,16,1]{0,1,2:T(8,128)S(1)} copy(f32[16,16,1]{2,1,0:T(8,128)} %get-tuple-element.43) | data formatting | bytes 2048 | tf_op jit(solution)/shard_map/squeeze | solution.py:123
  26.8 1.1 %copy.193 = f32[16,16,1]{0,1,2:T(8,128)S(1)} copy(f32[16,16,1]{2,1,0:T(8,128)} %get-tuple-element.51) | data formatting | bytes 2048 | tf_op jit(solution)/shard_map/mul | solution.py:98
  28.3 36.0 %all-reduce.3 = f32[16,48]{0,1:T(8,128)S(1)} all-reduce(f32[16,48]{0,1:T(8,128)S(1)} %fusion.54), channel_id=2, replica_groups=mesh['strike'=8,'depth'=4] {'strike'}, use_global_device_ids=true, to_apply=%region_0.1.clone | all-reduce | flops 768 | bytes 6144
  64.6 30.6 %all-gather = f32[8,6,16]{2,1,0:T(8,128)S(1)} all-gather(f32[1,6,16]{2,1,0:T(8,128)S(1)} %bitcast.174), channel_id=1, replica_groups=mesh['strike'=8,'depth'=4] {'strike'}, dimensions={0}, use_global_device_ids=true | all-gather | bytes 3456 | tf_op jit(solution)/shard_map/all_gather | solution.py:113
  95.4 1.1 %copy.198 = f32[16,16,1]{0,1,2:T(8,128)S(1)} copy(f32[16,16,1]{2,1,0:T(8,128)} %get-tuple-element.44) | data formatting | bytes 2048 | tf_op jit(solution)/shard_map/squeeze | solution.py:122
  96.6 0.8 copy.189
  97.4 0.8 copy.192
  98.2 1.0 scatter.6
  99.2 2.1 %scatter.9 = f32[1,16,16,256]{3,2,1,0:T(8,128)S(1)} dynamic-update-slice(f32[1,16,16,256]{3,2,1,0:T(8,128)S(1)} %scatter.6, f32[1,16,16,1]{3,2,1,0:T(8,128)} %copy.192, s32[]{:T(128)} %constant.89.clone.1, s32[]{:T(128)} %constant.89.clone.1, s32[]{:T(128)} %constant.89.clone.1, s32[]{:T(128)} %constant.111.clone.1) | dynamic-update-slice | bytes 2052 | tf_op jit(solution)/shard_map/scatter | solution.py:126
  101.4 1.4 %fusion.27 = f32[1,16,16,256]{3,2,1,0:T(8,128)S(1)} fusion(f32[16,16,256]{2,1,0:T(8,128)S(1)} %get-tuple-element.40, f32[16,20,256]{2,1,0:T(8,128)S(1)} %get-tuple-element.34, f32[5,2,16,256]{3,2,1,0:T(8,128)S(1)} %collective-permute-done, f32[4,16,16,256]{3,2,1,0:T(8,128)S(1)} %slice.262, f32[1,16,16,256]{3,2,1,0:T(8,128)S(1)} %get-tuple-element.39, ...), kind=kLoop, calls=%fused_computation.44 | loop fusion | flops 2424832 | bytes 3997696 | tf_op jit(solution)/shard_map/stack | solution.py:127
  102.8 1.4 %fusion.17 = f32[1,16,16,256]{3,2,1,0:T(8,128)S(1)} fusion(f32[16,16,256]{2,1,0:T(8,128)S(1)} %get-tuple-element.38, f32[16,20,256]{2,1,0:T(8,128)S(1)} %get-tuple-element.33, f32[5,2,16,256]{3,2,1,0:T(8,128)S(1)} %collective-permute-done, f32[4,16,16,256]{3,2,1,0:T(8,128)S(1)} %slice.262, f32[1,16,16,256]{3,2,1,0:T(8,128)S(1)} %get-tuple-element.39, ...), kind=kLoop, calls=%fused_computation.34 | loop fusion | flops 2424832 | bytes 3997696 | tf_op jit(solution)/shard_map/stack | solution.py:127
  104.2 0.9 pad_maximum_fusion
  (29 shorter events, 1.6 us)
Async XLA Ops:
  0.6 2.1 %copy-start = (f32[6,16,16,256]{3,2,1,0:T(8,128)S(1)}, f32[6,16,16,256]{3,2,1,0:T(8,128)}, u32[]{:S(2)}) copy-start(f32[6,16,16,256]{3,2,1,0:T(8,128)} %param.10) | copy-start | bytes 4718596
  2.7 6.2 %copy-start.6 = (u32[32]{0:T(128)S(1)}, u32[32]{0:T(128)}, u32[]{:S(2)}) copy-start(u32[32]{0:T(128)} %constant.121) | copy-start | bytes 388
  2.8 15.8 %copy-start.4 = (f32[4,16,6]{1,0,2:T(4,128)S(1)}, f32[4,16,6]{1,0,2:T(4,128)}, u32[]{:S(2)}) copy-start(f32[4,16,6]{1,0,2:T(4,128)} %param.13) | copy-start | bytes 4612
  2.8 7.8 %collective-permute-start.1 = (f32[5,2,16,256]{3,2,1,0:T(8,128)S(1)}, f32[5,2,16,256]{3,2,1,0:T(8,128)S(1)}, u32[]{:S(2)}, u32[]{:S(2)}) collective-permute-start(f32[5,2,16,256]{3,2,1,0:T(8,128)S(1)} %get-tuple-element.42), channel_id=1, source_target_pairs={{4,0},{8,4},{12,8},{16,12},{20,16},{24,20},{28,24},{5,1},{9,5},{13... | collective-permute-start | bytes 491528 | tf_op jit(solution)/shard_map/ppermute | solution.py:20
  4.1 10.0 %collective-permute-start = (f32[5,2,16,256]{3,2,1,0:T(8,128)S(1)}, f32[5,2,16,256]{3,2,1,0:T(8,128)S(1)}, u32[]{:S(2)}, u32[]{:S(2)}) collective-permute-start(f32[5,2,16,256]{3,2,1,0:T(8,128)S(1)} %get-tuple-element.41), channel_id=1, source_target_pairs={{0,4},{4,8},{8,12},{12,16},{16,20},{20,24},{24,28},{1,5},{5,9},{9,... | collective-permute-start | bytes 491528 | tf_op jit(solution)/shard_map/ppermute | solution.py:19
  14.3 5.3 %collective-permute-start.3 = (f32[5,20,2,256]{3,2,1,0:T(2,128)S(1)}, f32[5,20,2,256]{3,2,1,0:T(2,128)S(1)}, u32[]{:S(2)}, u32[]{:S(2)}) collective-permute-start(f32[5,20,2,256]{3,2,1,0:T(2,128)S(1)} %get-tuple-element.36), channel_id=1, source_target_pairs={{1,0},{2,1},{3,2},{5,4},{6,5},{7,6},{9,8},{10,9},{11,10},{13,12},{... | collective-permute-start | bytes 614408 | tf_op jit(solution)/shard_map/ppermute | solution.py:20
  16.3 7.1 %collective-permute-start.2 = (f32[5,20,2,256]{3,2,1,0:T(2,128)S(1)}, f32[5,20,2,256]{3,2,1,0:T(2,128)S(1)}, u32[]{:S(2)}, u32[]{:S(2)}) collective-permute-start(f32[5,20,2,256]{3,2,1,0:T(2,128)S(1)} %get-tuple-element.35), channel_id=1, source_target_pairs={{0,1},{1,2},{2,3},{4,5},{5,6},{6,7},{8,9},{9,10},{10,11},{12,13},{... | collective-permute-start | bytes 614408 | tf_op jit(solution)/shard_map/ppermute | solution.py:19
  18.6 5.0 %copy-start.1 = (s32[16,16,256]{2,1,0:T(8,128)S(1)}, s32[16,16,256]{2,1,0:T(8,128)}, u32[]{:S(2)}) copy-start(s32[16,16,256]{2,1,0:T(8,128)} %param.11) | copy-start | bytes 786436
  18.7 5.0 %copy-start.2 = (f32[16,16,256]{2,1,0:T(8,128)S(1)}, f32[16,16,256]{2,1,0:T(8,128)}, u32[]{:S(2)}) copy-start(f32[16,16,256]{2,1,0:T(8,128)} %get-tuple-element.37) | copy-start | bytes 786436
  23.6 4.5 %copy-start.5 = (s32[48]{0:T(128)S(1)}, s32[48]{0:T(128)}, u32[]{:S(2)}) copy-start(s32[48]{0:T(128)} %param.12) | copy-start | bytes 580
  64.6 38.2 %copy-start.3 = (f32[16,6]{0,1:T(8,128)}, f32[16,6]{0,1:T(8,128)S(1)}, u32[]{:S(2)}) copy-start(f32[16,6]{0,1:T(8,128)S(1)} %fusion.103) | copy-start | bytes 1156
where the time goes:
time: 106 us; the launch traced here: 105 us
  blocking collectives  66.6 us (63%)
  local copies, waits for them, and re-layouts  11.2 us (11%)
  starting transfers between devices  10.2 us (10%)
  waiting for transfers between devices  8.72 us (8%)
  other arithmetic  6.48 us (6%)
  between operations  1.5 us (1%)
    unnamed x1, blocking collectives  36 us
    all_gather x1, blocking collectives, per_device(): slip_all = lax.all_gather(slip_own, 'strike', axis=1, tiled=True)  30.6 us
    ppermute x2, waiting for transfers between devices, with_halo(): before = lax.ppermute(last, axis, up)  7.27 us
    ppermute x2, starting transfers between devices, with_halo(): before = lax.ppermute(last, axis, up)  6.83 us
    another operation x4, other arithmetic, per_device(): return (jnp.stack([vx, vy, vz]), slip_own)  3.81 us
    ppermute x2, starting transfers between devices, with_halo(): after = lax.ppermute(first, axis, down)  3.36 us
    scatter x1, local copies, waits for them, and re-layouts, per_device(): vx.at[:, :, row - 1]  2.14 us
  transfers between devices with their start and end apart: 4, of which 4 were waited for; matrix products, arithmetic and copies ran while one was open for 1% of the time, Pallas kernels for 0%

commit v1 on v0

--- a/solution.py
+++ b/solution.py
@@ -110,7 +110,16 @@
         tiled=True,
     )
     slip_own = friction(owned, fault_params)
-    slip_all = lax.all_gather(slip_own, "strike", axis=1, tiled=True)
+    ways = lax.axis_size("strike")
+    up_2 = [(d, (d + 1) % ways) for d in range(ways)]
+    down_2 = [(d, (d - 1) % ways) for d in range(ways)]
+    earlier, later = ([slip_own], [slip_own])
+    for _ in range(ways // 2):
+        earlier.append(lax.ppermute(earlier[-1], "strike", up_2))
+    for _ in range((ways - 1) // 2):
+        later.append(lax.ppermute(later[-1], "strike", down_2))
+    line = jnp.concatenate([*earlier[::-1], *later[1:]], axis=1)
+    slip_all = jnp.roll(line, (lax.axis_index("strike") - ways // 2) * slip_own.shape[1], axis=1)
     slip_tile = lax.dynamic_slice(
         jnp.dot(
             slip_all, selector, precision=lax.Precision.HIGHEST, preferred_element_type=jnp.float32

time: 106 us -> 92 us (0.87)
  blocking collectives: 66.6 us -> 36 us
  starting transfers between devices: 10.2 us -> 24.6 us
  waiting for transfers between devices: 8.72 us -> 14.7 us
  local copies, waits for them, and re-layouts: 11.2 us -> 7.15 us
    all_gather x1 -> x0, blocking collectives: 30.6 us -> none  [per_device(): slip_all = lax.all_gather(slip_own, 'strike', axis=1, tiled=True)]
    ppermute x0 -> x7, starting transfers between devices: none -> 14.4 us  [the longest x3 14.3 us: per_device(): later.append(lax.ppermute(later[-1], 'strike', down_2))]
    ppermute x0 -> x7, waiting for transfers between devices: none -> 6 us  [the longest x4 5.19 us: per_device(): earlier.append(lax.ppermute(earlier[-1], 'strike', up_2))]
    another operation x2, local copies, waits for them, and re-layouts: 1.65 us -> 0.36 us  [per_device(): return (jnp.stack([vx, vy, vz]), slip_own)]
  transfers between devices with their start and end apart: 4 -> 11, of which waited for: 4 -> 8; matrix products, arithmetic and copies ran while one was open for 1% -> 7% of each run, Pallas kernels for 0% -> 0%
where the time goes in v1:
time: 92 us; the launch traced here: 91.6 us
  blocking collectives  36 us (39%)
  starting transfers between devices  24.6 us (27%)
  waiting for transfers between devices  14.7 us (16%)
  local copies, waits for them, and re-layouts  7.15 us (8%)
  other arithmetic  7.14 us (8%)
  between operations  1.57 us (2%)
    unnamed x1, blocking collectives  36 us
    ppermute x3, starting transfers between devices, per_device(): later.append(lax.ppermute(later[-1], 'strike', down_2))  14.3 us
    ppermute x2, waiting for transfers between devices, with_halo(): before = lax.ppermute(last, axis, up)  7.27 us
    ppermute x2, starting transfers between devices, with_halo(): before = lax.ppermute(last, axis, up)  6.83 us
    ppermute x4, waiting for transfers between devices, per_device(): earlier.append(lax.ppermute(earlier[-1], 'strike', up_2))  5.19 us
    another operation x4, other arithmetic, per_device(): return (jnp.stack([vx, vy, vz]), slip_own)  4.48 us
    ppermute x2, starting transfers between devices, with_halo(): after = lax.ppermute(first, axis, down)  3.36 us
    squeeze x1, local copies, waits for them, and re-layouts, per_device(): stress[3]  2.08 us
  transfers between devices with their start and end apart: 11, of which 8 were waited for; matrix products, arithmetic and copies ran while one was open for 7% of the time, Pallas kernels for 0%

profile of v1, /device:TPU:2, one launch (start us, length us, event | category | flops | bytes accessed | tf_op | source)
XLA Modules:
  0.0 91.6 jit_solution(6060813623670643838)
XLA Ops:
  0.6 2.1 %slice_bitcast_fusion.2 = (f32[16,16,256]{2,1,0:T(8,128)S(1)}, f32[16,16,256]{2,1,0:T(8,128)S(1)}, f32[1,16,16,256]{3,2,1,0:T(8,128)S(1)}, f32[16,16,256]{2,1,0:T(8,128)}) fusion(f32[6,16,16,256]{3,2,1,0:T(8,128)} %param.10), kind=kLoop, calls=%fused_computation.87 | loop fusion | bytes 2097152 | tf_op jit(solution)/shard_map/squeeze | solution.py:80
  2.8 1.3 %collective-permute-start.1 = (f32[5,2,16,256]{3,2,1,0:T(8,128)S(1)}, f32[5,2,16,256]{3,2,1,0:T(8,128)S(1)}, u32[]{:S(2)}, u32[]{:S(2)}) collective-permute-start(f32[5,2,16,256]{3,2,1,0:T(8,128)S(1)} %get-tuple-element.40), channel_id=1, source_target_pairs={{4,0},{8,4},{12,8},{16,12},{20,16},{24,20},{28,24},{5,1},{9,5},{13... | collective-permute-start | bytes 491528 | tf_op jit(solution)/shard_map/ppermute | solution.py:20
  4.1 4.6 %collective-permute-start = (f32[5,2,16,256]{3,2,1,0:T(8,128)S(1)}, f32[5,2,16,256]{3,2,1,0:T(8,128)S(1)}, u32[]{:S(2)}, u32[]{:S(2)}) collective-permute-start(f32[5,2,16,256]{3,2,1,0:T(8,128)S(1)} %get-tuple-element.39), channel_id=1, source_target_pairs={{0,4},{4,8},{8,12},{12,16},{16,20},{20,24},{24,28},{1,5},{5,9},{9,... | collective-permute-start | bytes 491528 | tf_op jit(solution)/shard_map/ppermute | solution.py:19
  8.9 0.6 dynamic-slice.16
  10.2 0.5 collective-permute-done.1
  10.7 3.4 %collective-permute-done = f32[5,2,16,256]{3,2,1,0:T(8,128)S(1)} collective-permute-done((f32[5,2,16,256]{3,2,1,0:T(8,128)S(1)}, f32[5,2,16,256]{3,2,1,0:T(8,128)S(1)}, u32[]{:S(2)}, u32[]{:S(2)}) %collective-permute-start) | collective-permute-done | bytes 163872 | tf_op jit(solution)/shard_map/ppermute | solution.py:19
  14.3 2.1 %collective-permute-start.3 = (f32[5,20,2,256]{3,2,1,0:T(2,128)S(1)}, f32[5,20,2,256]{3,2,1,0:T(2,128)S(1)}, u32[]{:S(2)}, u32[]{:S(2)}) collective-permute-start(f32[5,20,2,256]{3,2,1,0:T(2,128)S(1)} %get-tuple-element.34), channel_id=1, source_target_pairs={{1,0},{2,1},{3,2},{5,4},{6,5},{7,6},{9,8},{10,9},{11,10},{13,12},{... | collective-permute-start | bytes 614408 | tf_op jit(solution)/shard_map/ppermute | solution.py:20
  16.3 2.3 %collective-permute-start.2 = (f32[5,20,2,256]{3,2,1,0:T(2,128)S(1)}, f32[5,20,2,256]{3,2,1,0:T(2,128)S(1)}, u32[]{:S(2)}, u32[]{:S(2)}) collective-permute-start(f32[5,20,2,256]{3,2,1,0:T(2,128)S(1)} %get-tuple-element.33), channel_id=1, source_target_pairs={{0,1},{1,2},{2,3},{4,5},{5,6},{6,7},{8,9},{9,10},{10,11},{12,13},{... | collective-permute-start | bytes 614408 | tf_op jit(solution)/shard_map/ppermute | solution.py:19
  18.7 0.9 %collective-permute-done.3 = f32[5,20,2,256]{3,2,1,0:T(2,128)S(1)} collective-permute-done((f32[5,20,2,256]{3,2,1,0:T(2,128)S(1)}, f32[5,20,2,256]{3,2,1,0:T(2,128)S(1)}, u32[]{:S(2)}, u32[]{:S(2)}) %collective-permute-start.3) | collective-permute-done | bytes 204832 | tf_op jit(solution)/shard_map/ppermute | solution.py:20
  19.6 3.8 %collective-permute-done.2 = f32[5,20,2,256]{3,2,1,0:T(2,128)S(1)} collective-permute-done((f32[5,20,2,256]{3,2,1,0:T(2,128)S(1)}, f32[5,20,2,256]{3,2,1,0:T(2,128)S(1)}, u32[]{:S(2)}, u32[]{:S(2)}) %collective-permute-start.2) | collective-permute-done | bytes 204832 | tf_op jit(solution)/shard_map/ppermute | solution.py:19
  23.6 1.3 %fusion.7 = (f32[16,16,256]{2,1,0:T(8,128)S(1)}, f32[16,16,256]{2,1,0:T(8,128)S(1)}) fusion(f32[16,16,256]{2,1,0:T(8,128)S(1)} %get-tuple-element.35, f32[16,20,256]{2,1,0:T(8,128)S(1)} %get-tuple-element.30, f32[3,16,16,256]{3,2,1,0:T(8,128)} %param.9, s32[16,16,256]{2,1,0:T(8,128)S(1)} %copy-done.1, f32[4,16,16,256]{3,2,1,0:T(8,128)S(1)} %slice.262, ...), kind=kLoop, calls=%fused_computation.24 | loop fusion | flops 2424832 | bytes 3997696 | tf_op jit(solution)/shard_map/add | solution.py:79
  25.0 0.8 fusion.110
  25.9 0.2 dynamic_update_slice.3
  26.4 36.0 %all-reduce.3 = f32[16,48]{0,1:T(8,128)S(1)} all-reduce(f32[16,48]{0,1:T(8,128)S(1)} %fusion.54), channel_id=2, replica_groups=mesh['strike'=8,'depth'=4] {'strike'}, use_global_device_ids=true, to_apply=%region_0.1.clone | all-reduce | flops 768 | bytes 6144
  62.7 4.7 %collective-permute-start.8 = (f32[16,6]{0,1:T(8,128)S(1)}, f32[16,6]{0,1:T(8,128)S(1)}, u32[]{:S(2)}, u32[]{:S(2)}) collective-permute-start(f32[16,6]{0,1:T(8,128)S(1)} %fusion.104), channel_id=1, source_target_pairs={{0,28},{4,0},{8,4},{12,8},{16,12},{20,16},{24,20},{28,24},{1,29},{... | collective-permute-start | bytes 1160 | tf_op jit(solution)/shard_map/ppermute | solution.py:120
  67.4 2.0 %fusion.27 = f32[1,16,16,256]{3,2,1,0:T(8,128)S(1)} fusion(f32[16,16,256]{2,1,0:T(8,128)} %get-tuple-element.38, f32[16,20,256]{2,1,0:T(8,128)S(1)} %get-tuple-element.32, f32[5,2,16,256]{3,2,1,0:T(8,128)S(1)} %collective-permute-done, f32[4,16,16,256]{3,2,1,0:T(8,128)S(1)} %slice.262, f32[1,16,16,256]{3,2,1,0:T(8,128)S(1)} %get-tuple-element.37, ...), kind=kLoop, calls=%fused_computation.44 | loop fusion | flops 2424832 | bytes 3997696 | tf_op jit(solution)/shard_map/stack | solution.py:136
  69.5 1.4 %fusion.17 = f32[1,16,16,256]{3,2,1,0:T(8,128)S(1)} fusion(f32[16,16,256]{2,1,0:T(8,128)S(1)} %get-tuple-element.36, f32[16,20,256]{2,1,0:T(8,128)S(1)} %get-tuple-element.31, f32[5,2,16,256]{3,2,1,0:T(8,128)S(1)} %collective-permute-done, f32[4,16,16,256]{3,2,1,0:T(8,128)S(1)} %slice.262, f32[1,16,16,256]{3,2,1,0:T(8,128)S(1)} %get-tuple-element.37, ...), kind=kLoop, calls=%fused_computation.34 | loop fusion | flops 2424832 | bytes 3997696 | tf_op jit(solution)/shard_map/stack | solution.py:136
  70.9 4.7 %collective-permute-start.9 = (f32[16,6]{0,1:T(8,128)S(1)}, f32[16,6]{0,1:T(8,128)S(1)}, u32[]{:S(2)}, u32[]{:S(2)}) collective-permute-start(f32[16,6]{0,1:T(8,128)S(1)} %collective-permute-done.8), channel_id=1, source_target_pairs={{0,28},{4,0},{8,4},{12,8},{16,12},{20,16},{24,20},{28,24},{1,29},{... | collective-permute-start | bytes 1160 | tf_op jit(solution)/shard_map/ppermute | solution.py:120
  75.9 1.1 %copy.281 = f32[16,16,1]{0,1,2:T(8,128)S(1)} copy(f32[16,16,1]{2,1,0:T(8,128)} %get-tuple-element.41) | data formatting | bytes 2048 | tf_op jit(solution)/shard_map/squeeze | solution.py:132
  77.1 4.9 %collective-permute-start.10 = (f32[16,6]{0,1:T(8,128)S(1)}, f32[16,6]{0,1:T(8,128)S(1)}, u32[]{:S(2)}, u32[]{:S(2)}) collective-permute-start(f32[16,6]{0,1:T(8,128)S(1)} %collective-permute-done.9), channel_id=1, source_target_pairs={{0,28},{4,0},{8,4},{12,8},{16,12},{20,16},{24,20},{28,24},{1,29},{... | collective-permute-start | bytes 1160 | tf_op jit(solution)/shard_map/ppermute | solution.py:120
  82.5 0.8 collective-permute-done.10
  83.4 5.0 %collective-permute-done.7 = f32[16,6]{0,1:T(8,128)S(1)} collective-permute-done((f32[16,6]{0,1:T(8,128)S(1)}, f32[16,6]{0,1:T(8,128)S(1)}, u32[]{:S(2)}, u32[]{:S(2)}) %collective-permute-start.7) | collective-permute-done | bytes 416 | tf_op jit(solution)/shard_map/ppermute | solution.py:118
  89.4 1.2 %scatter.9 = f32[1,16,16,256]{3,2,1,0:T(8,128)S(1)} dynamic-update-slice(f32[1,16,16,256]{3,2,1,0:T(8,128)S(1)} %scatter.6, f32[1,16,16,1]{3,2,1,0:T(8,128)S(1)} %copy.274, s32[]{:T(128)} %constant.108.clone.1, s32[]{:T(128)} %constant.108.clone.1, s32[]{:T(128)} %constant.108.clone.1, s32[]{:T(128)} %constant.133.clone.1) | dynamic-update-slice | bytes 2052 | tf_op jit(solution)/shard_map/scatter | solution.py:135
  90.7 0.9 %pad_maximum_fusion = f32[3,16,16,256]{3,2,1,0:T(8,128)} fusion(f32[1,16,16,256]{3,2,1,0:T(8,128)S(1)} %fusion.27, f32[1,16,16,256]{3,2,1,0:T(8,128)S(1)} %fusion.17, f32[1,16,16,256]{3,2,1,0:T(8,128)S(1)} %scatter.9), kind=kLoop, calls=%fused_computation | loop fusion | flops 393216 | bytes 1572864 | tf_op jit(solution)/shard_map/stack | solution.py:136
  (50 shorter events, 3.3 us)
Async XLA Ops:
  0.6 2.1 %copy-start = (f32[6,16,16,256]{3,2,1,0:T(8,128)S(1)}, f32[6,16,16,256]{3,2,1,0:T(8,128)}, u32[]{:S(2)}) copy-start(f32[6,16,16,256]{3,2,1,0:T(8,128)} %param.10) | copy-start | bytes 4718596
  2.8 6.2 %copy-start.6 = (u32[32]{0:T(128)S(1)}, u32[32]{0:T(128)}, u32[]{:S(2)}) copy-start(u32[32]{0:T(128)} %constant.143) | copy-start | bytes 388
  2.8 15.8 %copy-start.4 = (f32[4,16,6]{1,0,2:T(4,128)S(1)}, f32[4,16,6]{1,0,2:T(4,128)}, u32[]{:S(2)}) copy-start(f32[4,16,6]{1,0,2:T(4,128)} %param.13) | copy-start | bytes 4612
  2.8 7.8 %collective-permute-start.1 = (f32[5,2,16,256]{3,2,1,0:T(8,128)S(1)}, f32[5,2,16,256]{3,2,1,0:T(8,128)S(1)}, u32[]{:S(2)}, u32[]{:S(2)}) collective-permute-start(f32[5,2,16,256]{3,2,1,0:T(8,128)S(1)} %get-tuple-element.40), channel_id=1, source_target_pairs={{4,0},{8,4},{12,8},{16,12},{20,16},{24,20},{28,24},{5,1},{9,5},{13... | collective-permute-start | bytes 491528 | tf_op jit(solution)/shard_map/ppermute | solution.py:20
  4.1 10.0 %collective-permute-start = (f32[5,2,16,256]{3,2,1,0:T(8,128)S(1)}, f32[5,2,16,256]{3,2,1,0:T(8,128)S(1)}, u32[]{:S(2)}, u32[]{:S(2)}) collective-permute-start(f32[5,2,16,256]{3,2,1,0:T(8,128)S(1)} %get-tuple-element.39), channel_id=1, source_target_pairs={{0,4},{4,8},{8,12},{12,16},{16,20},{20,24},{24,28},{1,5},{5,9},{9,... | collective-permute-start | bytes 491528 | tf_op jit(solution)/shard_map/ppermute | solution.py:19
  14.3 5.3 %collective-permute-start.3 = (f32[5,20,2,256]{3,2,1,0:T(2,128)S(1)}, f32[5,20,2,256]{3,2,1,0:T(2,128)S(1)}, u32[]{:S(2)}, u32[]{:S(2)}) collective-permute-start(f32[5,20,2,256]{3,2,1,0:T(2,128)S(1)} %get-tuple-element.34), channel_id=1, source_target_pairs={{1,0},{2,1},{3,2},{5,4},{6,5},{7,6},{9,8},{10,9},{11,10},{13,12},{... | collective-permute-start | bytes 614408 | tf_op jit(solution)/shard_map/ppermute | solution.py:20
  16.3 7.1 %collective-permute-start.2 = (f32[5,20,2,256]{3,2,1,0:T(2,128)S(1)}, f32[5,20,2,256]{3,2,1,0:T(2,128)S(1)}, u32[]{:S(2)}, u32[]{:S(2)}) collective-permute-start(f32[5,20,2,256]{3,2,1,0:T(2,128)S(1)} %get-tuple-element.33), channel_id=1, source_target_pairs={{0,1},{1,2},{2,3},{4,5},{5,6},{6,7},{8,9},{9,10},{10,11},{12,13},{... | collective-permute-start | bytes 614408 | tf_op jit(solution)/shard_map/ppermute | solution.py:19
  18.7 5.0 %copy-start.1 = (s32[16,16,256]{2,1,0:T(8,128)S(1)}, s32[16,16,256]{2,1,0:T(8,128)}, u32[]{:S(2)}) copy-start(s32[16,16,256]{2,1,0:T(8,128)} %param.11) | copy-start | bytes 786436
  23.6 2.5 %copy-start.5 = (s32[48]{0:T(128)S(1)}, s32[48]{0:T(128)}, u32[]{:S(2)}) copy-start(s32[48]{0:T(128)} %param.12) | copy-start | bytes 580
  62.6 13.2 %copy-start.3 = (f32[16,6]{0,1:T(8,128)}, f32[16,6]{0,1:T(8,128)S(1)}, u32[]{:S(2)}) copy-start(f32[16,6]{0,1:T(8,128)S(1)} %fusion.104) | copy-start | bytes 1156
  62.6 6.8 %collective-permute-start.4 = (f32[16,6]{0,1:T(8,128)S(1)}, f32[16,6]{0,1:T(8,128)S(1)}, u32[]{:S(2)}, u32[]{:S(2)}) collective-permute-start(f32[16,6]{0,1:T(8,128)S(1)} %fusion.104), channel_id=1, source_target_pairs={{0,4},{4,8},{8,12},{12,16},{16,20},{20,24},{24,28},{28,0},{1,5},{5... | collective-permute-start | bytes 1160 | tf_op jit(solution)/shard_map/ppermute | solution.py:118
  62.7 8.3 %collective-permute-start.8 = (f32[16,6]{0,1:T(8,128)S(1)}, f32[16,6]{0,1:T(8,128)S(1)}, u32[]{:S(2)}, u32[]{:S(2)}) collective-permute-start(f32[16,6]{0,1:T(8,128)S(1)} %fusion.104), channel_id=1, source_target_pairs={{0,28},{4,0},{8,4},{12,8},{16,12},{20,16},{24,20},{28,24},{1,29},{... | collective-permute-start | bytes 1160 | tf_op jit(solution)/shard_map/ppermute | solution.py:120
  69.4 6.4 %collective-permute-start.5 = (f32[16,6]{0,1:T(8,128)S(1)}, f32[16,6]{0,1:T(8,128)S(1)}, u32[]{:S(2)}, u32[]{:S(2)}) collective-permute-start(f32[16,6]{0,1:T(8,128)S(1)} %collective-permute-done.4), channel_id=1, source_target_pairs={{0,4},{4,8},{8,12},{12,16},{16,20},{20,24},{24,28},{28,0},{1,5},{5... | collective-permute-start | bytes 1160 | tf_op jit(solution)/shard_map/ppermute | solution.py:118
  69.5 7.5 %copy-start.2 = (f32[16,16,1]{2,1,0:T(8,128)S(1)}, f32[16,16,1]{2,1,0:T(8,128)}, u32[]{:S(2)}) copy-start(f32[16,16,1]{2,1,0:T(8,128)} %get-tuple-element.42) | copy-start | bytes 3076
  70.9 6.2 %collective-permute-start.9 = (f32[16,6]{0,1:T(8,128)S(1)}, f32[16,6]{0,1:T(8,128)S(1)}, u32[]{:S(2)}, u32[]{:S(2)}) collective-permute-start(f32[16,6]{0,1:T(8,128)S(1)} %collective-permute-done.8), channel_id=1, source_target_pairs={{0,28},{4,0},{8,4},{12,8},{16,12},{20,16},{24,20},{28,24},{1,29},{... | collective-permute-start | bytes 1160 | tf_op jit(solution)/shard_map/ppermute | solution.py:120
  75.8 6.3 %collective-permute-start.6 = (f32[16,6]{0,1:T(8,128)S(1)}, f32[16,6]{0,1:T(8,128)S(1)}, u32[]{:S(2)}, u32[]{:S(2)}) collective-permute-start(f32[16,6]{0,1:T(8,128)S(1)} %collective-permute-done.5), channel_id=1, source_target_pairs={{0,4},{4,8},{8,12},{12,16},{16,20},{20,24},{24,28},{28,0},{1,5},{5... | collective-permute-start | bytes 1160 | tf_op jit(solution)/shard_map/ppermute | solution.py:118
  77.1 6.2 %collective-permute-start.10 = (f32[16,6]{0,1:T(8,128)S(1)}, f32[16,6]{0,1:T(8,128)S(1)}, u32[]{:S(2)}, u32[]{:S(2)}) collective-permute-start(f32[16,6]{0,1:T(8,128)S(1)} %collective-permute-done.9), channel_id=1, source_target_pairs={{0,28},{4,0},{8,4},{12,8},{16,12},{20,16},{24,20},{28,24},{1,29},{... | collective-permute-start | bytes 1160 | tf_op jit(solution)/shard_map/ppermute | solution.py:120
  82.1 6.3 %collective-permute-start.7 = (f32[16,6]{0,1:T(8,128)S(1)}, f32[16,6]{0,1:T(8,128)S(1)}, u32[]{:S(2)}, u32[]{:S(2)}) collective-permute-start(f32[16,6]{0,1:T(8,128)S(1)} %collective-permute-done.6), channel_id=1, source_target_pairs={{0,4},{4,8},{8,12},{12,16},{16,20},{20,24},{24,28},{28,0},{1,5},{5... | collective-permute-start | bytes 1160 | tf_op jit(solution)/shard_map/ppermute | solution.py:118
